TPU v7x, 512 devices: a whole 4x8x8 slice. The times are simulated.
512 devices in a mesh: dom: 32 (over z, x), band: 16 (over y, core).
Axes of the slice: x: 4, y: 8, z: 8, core: 2. Of those that a mesh axis runs over, the one named last changes fastest.
Arguments:
- waves: float32 [256, 131072], P('band', 'dom'), may hold values from -6 to 6
- potential: float32 [131072], P('dom'), may hold values from 0 to 4
- atom_points: int32 [128, 256], P('dom'), may hold values from 0 to 4095
- projectors: float32 [128, 8, 256], P('dom'), may hold values from -0.75 to 0.75
- coupling: float32 [128, 8, 8], P('dom'), may hold values from -1 to 1
Outputs:
- ortho: float32 [256, 131072], P('band', 'dom')
Inputs may be any that keep to these rules, and one draw needn't show every extreme that they name: `atom_points`: an index of a point within the atom's own subdomain, repeats allowed.
All inputs are finite; a program needn't handle non-finite values.
Results may differ from a plain program's by a relative error of at most 0.0003.
Values sent between devices are 32-bit elements; how exact they have to be, the bound alone decides.
A program may use at most 64 MiB of HBM per device.

v0:
```python
import jax
import jax.numpy as jnp
from jax import lax
from jax.sharding import PartitionSpec as P

CUBE = 16
high = lax.Precision.HIGHEST


def passed_along(value, axis, by):
    size = lax.axis_size(axis)
    pairs = [(i, i + by) for i in range(size) if 0 <= i + by < size]
    return lax.ppermute(value, axis, pairs)


def shifted(face, offset):
    return passed_along(face, "dom", offset)


def laplace(grid, coords, counts, strides):
    total = -7.5 * grid
    for dim in range(3):
        axis = dim + 1
        lower_face = lax.slice_in_dim(grid, 0, 2, axis=axis)
        upper_face = lax.slice_in_dim(grid, CUBE - 2, CUBE, axis=axis)
        above = shifted(lower_face, -strides[dim]) * (coords[dim] < counts[dim] - 1).astype(
            jnp.float32
        )
        below = shifted(upper_face, strides[dim]) * (coords[dim] > 0).astype(jnp.float32)
        padded = jnp.concatenate([below, grid, above], axis=axis)

        def part(offset):
            return lax.slice_in_dim(padded, offset, offset + CUBE, axis=axis)

        total = total + 4.0 / 3.0 * (part(1) + part(3)) - 1.0 / 12.0 * (part(0) + part(4))
    return total


def nonlocal_one(values, points, proj, coup):
    picked = values[:, points]
    coef = jnp.einsum("aks,bas->bak", proj, picked, precision=high)
    mixed = jnp.einsum("akj,baj->bak", coup, coef, precision=high)
    spread = jnp.einsum("aks,bak->bas", proj, mixed, precision=high)
    return jnp.zeros_like(values).at[:, points.reshape(-1)].add(spread.reshape(values.shape[0], -1))


def local(waves, potential, atom_points, projectors, coupling):
    groups, local_points = waves.shape
    dom_count = lax.axis_size("dom")
    depth_z = 2
    depth_y = min(4, dom_count // 2)
    depth_x = dom_count // (depth_z * depth_y)
    where = lax.axis_index("dom")
    coords = (where // (depth_y * depth_z), where // depth_z % depth_y, where % depth_z)
    counts = (depth_x, depth_y, depth_z)
    strides = (depth_y * depth_z, depth_z, 1)

    def apply_h(values):
        grid = values.reshape(groups, CUBE, CUBE, CUBE)
        kinetic = laplace(grid, coords, counts, strides).reshape(groups, local_points)
        extra = nonlocal_one(values, atom_points, projectors, coupling)
        return -0.5 * kinetic + potential[None, :] * values + extra

    first = (apply_h(waves) - 6.0 * waves) / 4.0
    filtered = 2.0 * (apply_h(first) - 6.0 * first) / 4.0 - waves
    pieces = lax.all_to_all(filtered, "band", split_axis=1, concat_axis=0, tiled=True)
    scale = 1.0 / (dom_count * local_points)
    partial_value = (
        jnp.dot(pieces, pieces.T, precision=high, preferred_element_type=jnp.float32) * scale
    )
    gram = lax.psum(partial_value, ("dom", "band"))
    lower = jnp.linalg.cholesky(gram)
    rotated = jax.scipy.linalg.solve_triangular(lower, pieces, lower=True)
    return lax.all_to_all(rotated, "band", split_axis=0, concat_axis=1, tiled=True)


def solution(mesh):
    placed = (
        P("band", "dom"),
        P("dom"),
        P("dom", None),
        P("dom", None, None),
        P("dom", None, None),
    )
    return jax.shard_map(
        local, mesh=mesh, in_specs=placed, out_specs=P("band", "dom"), check_vma=False
    )
```

profile of v0, /device:TPU:1, one launch (start us, length us, event | category | flops | bytes accessed | tf_op | source)
XLA Modules:
  0.0 548.6 jit_solution(12536738940076583858)
XLA Ops:
  14.0 4.6 collective-permute-start.4
  18.7 3.9 copy.105
  25.1 5.5 %collective-permute-start.2 = (f32[16,16,2,16]{3,2,1,0:T(2,128)}, f32[16,16,2,16]{3,2,1,0:T(2,128)}, u32[]{:S(2)}, u32[]{:S(2)}) collective-permute-start(f32[16,16,2,16]{3,2,1,0:T(2,128)} %get-tuple-element.31), channel_id=1, source_target_pairs={{0,32},{16,48},{32,64},{48,80},{64,96},{80,112},{96,128},{112,144}... | collective-permute-start | bytes 98312 | tf_op jit(solution)/shard_map/ppermute | solution.py:13
  32.9 9.7 %collective-permute-start = (f32[16,2,16,16]{3,2,1,0:T(8,128)}, f32[16,2,16,16]{3,2,1,0:T(8,128)}, u32[]{:S(2)}, u32[]{:S(2)}) collective-permute-start(f32[16,2,16,16]{3,2,1,0:T(8,128)} %get-tuple-element.33), channel_id=1, source_target_pairs={{0,128},{16,144},{32,160},{48,176},{64,192},{80,208},{96,224},{112... | collective-permute-start | bytes 98312 | tf_op jit(solution)/shard_map/ppermute | solution.py:13
  44.6 4.4 gather_fusion
  64.2 7.2 %collective-permute-done.1 = f32[16,2,16,16]{3,2,1,0:T(8,128)} collective-permute-done((f32[16,2,16,16]{3,2,1,0:T(8,128)}, f32[16,2,16,16]{3,2,1,0:T(8,128)}, u32[]{:S(2)}, u32[]{:S(2)}) %collective-permute-start.1) | collective-permute-done | bytes 32800 | tf_op jit(solution)/shard_map/ppermute | solution.py:13
  72.3 8.1 %fusion.20 = f32[16,16,16,16]{3,2,1,0:T(8,128)} fusion(f32[16,16,16,16]{3,2,1,0:T(8,128)S(1)} %reshape.78, f32[16,2,16,16]{3,2,1,0:T(8,128)S(1)} %broadcast_multiply_fusion.10, f32[16,2,16,16]{3,2,1,0:T(8,128)S(1)} %broadcast_multiply_fusion.12, f32[16,16,2,16]{3,2,1,0:T(2,128)S(1)} %bitcast.110, f32[16,16,2,16]{3,2,1,0:T(2,128)S(1)} %bitcast.108, ...), kind=kLoop, calls=%fused_computation.42 | loop fusion | flops 2097152 | bytes 720896 | tf_op jit(solution)/shard_map/mul | solution.py:62
  84.3 7.6 %scatter_fusion = f32[16,4096]{0,1:T(8,128)S(1)} fusion(f32[16,4096]{0,1:T(8,128)S(1)} %copy.111, s32[1024]{0:T(1024)S(1)} %bitcast.121, f32[1024,16]{1,0:T(8,128)} %copy.112), kind=kCustom, calls=%fused_computation.2 | custom fusion | flops 16384 | bytes 200704 | tf_op jit(solution)/shard_map/scatter-add | solution.py:44
  105.0 3.9 copy.117
  110.2 4.0 collective-permute-start.8
  115.5 13.4 %collective-permute-start.6 = (f32[16,2,16,16]{3,2,1,0:T(8,128)}, f32[16,2,16,16]{3,2,1,0:T(8,128)}, u32[]{:S(2)}, u32[]{:S(2)}) collective-permute-start(f32[16,2,16,16]{3,2,1,0:T(8,128)} %get-tuple-element.27), channel_id=1, source_target_pairs={{0,128},{16,144},{32,160},{48,176},{64,192},{80,208},{96,224},{112... | collective-permute-start | bytes 98312 | tf_op jit(solution)/shard_map/ppermute | solution.py:13
  128.9 4.4 gather_fusion.1
  145.6 3.9 copy.119
  150.5 8.1 %fusion.9 = f32[16,16,16,16]{3,2,1,0:T(8,128)} fusion(f32[16,16,16,16]{3,2,1,0:T(8,128)S(1)} %reshape.81, f32[16,2,16,16]{3,2,1,0:T(8,128)S(1)} %broadcast_multiply_fusion.9, f32[16,2,16,16]{3,2,1,0:T(8,128)S(1)} %copy-done.2, f32[16,16,2,16]{3,2,1,0:T(2,128)S(1)} %bitcast.109, f32[16,16,2,16]{3,2,1,0:T(2,128)S(1)} %bitcast.107, ...), kind=kLoop, calls=%fused_computation.31 | loop fusion | flops 2097152 | bytes 720896 | tf_op jit(solution)/shard_map/mul | solution.py:62
  162.4 7.2 %scatter_fusion.1 = f32[16,4096]{0,1:T(8,128)S(1)} fusion(f32[16,4096]{0,1:T(8,128)S(1)} %copy.123, s32[1024]{0:T(1024)S(1)} %bitcast.122, f32[1024,16]{1,0:T(8,128)} %copy.124), kind=kCustom, calls=%fused_computation.3 | custom fusion | flops 16384 | bytes 200704 | tf_op jit(solution)/shard_map/scatter-add | solution.py:44
  170.9 9.0 %all-to-all-start = ((f32[16,16,256]{2,0,1:T(8,128)}), f32[16,16,256]{2,0,1:T(8,128)S(1)}, u32[]{:S(2)}, u32[]{:S(2)}) async-start(f32[16,16,256]{2,0,1:T(8,128)} %bitcast.90), calls=%async_computation | async-start | bytes 524288 | tf_op jit(solution)/shard_map/all_to_all | solution.py:66
  180.2 11.3 %all-to-all-done = f32[16,16,256]{2,0,1:T(8,128)S(1)} async-done(((f32[16,16,256]{2,0,1:T(8,128)}), f32[16,16,256]{2,0,1:T(8,128)S(1)}, u32[]{:S(2)}, u32[]{:S(2)}) %all-to-all-start) | async-done | bytes 262176 | tf_op jit(solution)/shard_map/all_to_all | solution.py:66
  192.7 267.4 %all-reduce.3.cloned.1.call-done = f32[256,256]{0,1:T(8,128)} async-done(((f32[256,256]{0,1:T(8,128)}), f32[256,256]{0,1:T(8,128)}) %all-reduce.3.cloned.1.call-update) | async-done | bytes 262160 | tf_op jit(solution)/shard_map/psum | solution.py:71
  462.2 11.7 %cholesky.50 = f32[128,128]{1,0:T(8,128)S(1)} custom-call(f32[128,128]{1,0:T(8,128)S(1)} %cholesky.118), custom_call_target="Cholesky" | custom-call | tf_op jit(solution)/shard_map/jit(cholesky)/cholesky | solution.py:72
  474.0 9.8 %custom-call.15 = f32[1,128,128]{1,2,0:T(8,128)S(1)} custom-call(f32[1,128,128]{2,1,0:T(8,128)S(1)} %get-tuple-element.40), custom_call_target="InvertDiagBlocksLowerTriangular" | custom-call | tf_op jit(solution)/shard_map/jit(cholesky)/cholesky | solution.py:72
  484.3 11.7 %cholesky.105 = f32[128,128]{1,0:T(8,128)S(1)} custom-call(f32[128,128]{1,0:T(8,128)S(1)} %convolution_subtract_fusion.1), custom_call_target="Cholesky" | custom-call | tf_op jit(solution)/shard_map/jit(cholesky)/cholesky | solution.py:72
  498.2 4.3 while.1
  502.5 19.7 %custom-call.16 = f32[2,128,128]{1,2,0:T(8,128)S(1)} custom-call(f32[2,128,128]{2,1,0:T(8,128)S(1)} %get-tuple-element.12), custom_call_target="InvertDiagBlocksLowerTriangular" | custom-call | tf_op jit(solution)/shard_map/jit(_solve_triangular)/triangular_solve | solution.py:73
  523.1 17.7 %all_to_all.38 = f32[16,16,256]{2,1,0:T(8,128)S(1)} all-to-all(f32[16,16,256]{2,1,0:T(8,128)S(1)} %bitcast.111), channel_id=1, replica_groups=mesh['dom'=32,'band'=16] {'band'}, dimensions={0} | all-to-all | bytes 524288 | tf_op jit(solution)/shard_map/all_to_all | solution.py:74
  (122 shorter events, 78.5 us)
Async XLA Ops:
  6.5 43.2 %copy-start = (f32[4,8,256]{2,1,0:T(8,128)S(1)}, f32[4,8,256]{2,1,0:T(8,128)}, u32[]{:S(2)}) copy-start(f32[4,8,256]{2,1,0:T(8,128)} %param.8) | copy-start | bytes 98308
  14.0 39.8 %collective-permute-start.4 = (f32[16,16,16,2]{2,1,3,0:T(8,128)S(1)}, f32[16,16,16,2]{2,1,3,0:T(8,128)}, u32[]{:S(2)}, u32[]{:S(2)}) collective-permute-start(f32[16,16,16,2]{2,1,3,0:T(8,128)S(1)} %copy.102), channel_id=1, source_target_pairs={{0,16},{16,32},{32,48},{48,64},{64,80},{80,96},{96,112},{112,128},... | collective-permute-start | bytes 98312 | tf_op jit(solution)/shard_map/ppermute | solution.py:13
  18.7 23.9 %copy-start.1 = (f32[16,4096]{1,0:T(8,128)S(1)}, f32[16,4096]{1,0:T(8,128)}, u32[]{:S(2)}) copy-start(f32[16,4096]{1,0:T(8,128)} %param.5) | copy-start | bytes 786436
  22.6 22.0 %copy-start.9 = (s32[4,256]{1,0:T(4,128)S(1)}, s32[4,256]{1,0:T(4,128)}, u32[]{:S(2)}) copy-start(s32[4,256]{1,0:T(4,128)} %param.7) | copy-start | bytes 12292
  22.6 32.2 %collective-permute-start.5 = (f32[16,16,16,2]{2,1,3,0:T(8,128)}, f32[16,16,16,2]{2,1,3,0:T(8,128)}, u32[]{:S(2)}, u32[]{:S(2)}) collective-permute-start(f32[16,16,16,2]{2,1,3,0:T(8,128)} %copy.105), channel_id=1, source_target_pairs={{16,0},{32,16},{48,32},{64,48},{80,64},{96,80},{112,96},{128,112},... | collective-permute-start | bytes 98312 | tf_op jit(solution)/shard_map/ppermute | solution.py:13
  25.1 26.4 %collective-permute-start.2 = (f32[16,16,2,16]{3,2,1,0:T(2,128)}, f32[16,16,2,16]{3,2,1,0:T(2,128)}, u32[]{:S(2)}, u32[]{:S(2)}) collective-permute-start(f32[16,16,2,16]{3,2,1,0:T(2,128)} %get-tuple-element.31), channel_id=1, source_target_pairs={{0,32},{16,48},{32,64},{48,80},{64,96},{80,112},{96,128},{112,144}... | collective-permute-start | bytes 98312 | tf_op jit(solution)/shard_map/ppermute | solution.py:13
  30.6 19.1 %copy-start.4 = (f32[4096]{0:T(1024)S(1)}, f32[4096]{0:T(1024)}, u32[]{:S(2)}) copy-start(f32[4096]{0:T(1024)} %param.6) | copy-start | bytes 49156
  30.6 23.1 %collective-permute-start.3 = (f32[16,16,2,16]{3,2,1,0:T(2,128)}, f32[16,16,2,16]{3,2,1,0:T(2,128)S(1)}, u32[]{:S(2)}, u32[]{:S(2)}) collective-permute-start(f32[16,16,2,16]{3,2,1,0:T(2,128)} %get-tuple-element.32), channel_id=1, source_target_pairs={{32,0},{48,16},{64,32},{80,48},{96,64},{112,80},{128,96},{144,112}... | collective-permute-start | bytes 98312 | tf_op jit(solution)/shard_map/ppermute | solution.py:13
  32.9 17.1 %copy-start.3 = (f32[4,8,8]{2,1,0:T(8,128)S(1)}, f32[4,8,8]{2,1,0:T(8,128)}, u32[]{:S(2)}) copy-start(f32[4,8,8]{2,1,0:T(8,128)} %param.9) | copy-start | bytes 3076
  32.9 23.6 %collective-permute-start = (f32[16,2,16,16]{3,2,1,0:T(8,128)}, f32[16,2,16,16]{3,2,1,0:T(8,128)}, u32[]{:S(2)}, u32[]{:S(2)}) collective-permute-start(f32[16,2,16,16]{3,2,1,0:T(8,128)} %get-tuple-element.33), channel_id=1, source_target_pairs={{0,128},{16,144},{32,160},{48,176},{64,192},{80,208},{96,224},{112... | collective-permute-start | bytes 98312 | tf_op jit(solution)/shard_map/ppermute | solution.py:13
  44.6 4.6 copy-start.7
  51.5 19.9 %collective-permute-start.1 = (f32[16,2,16,16]{3,2,1,0:T(8,128)}, f32[16,2,16,16]{3,2,1,0:T(8,128)}, u32[]{:S(2)}, u32[]{:S(2)}) collective-permute-start(f32[16,2,16,16]{3,2,1,0:T(8,128)} %get-tuple-element.34), channel_id=1, source_target_pairs={{128,0},{144,16},{160,32},{176,48},{192,64},{208,80},{224,96},{240... | collective-permute-start | bytes 98312 | tf_op jit(solution)/shard_map/ppermute | solution.py:13
  83.6 0.7 copy-start.5
  99.9 29.0 %copy-start.8 = (s32[1024]{0:T(1024)S(1)}, s32[1024]{0:T(1024)}, u32[]{:S(2)}) copy-start(s32[1024]{0:T(1024)} %copy-done.7) | copy-start | bytes 12292
  103.0 35.3 %collective-permute-start.10 = (f32[16,16,16,2]{2,1,3,0:T(8,128)S(1)}, f32[16,16,16,2]{2,1,3,0:T(8,128)}, u32[]{:S(2)}, u32[]{:S(2)}) collective-permute-start(f32[16,16,16,2]{2,1,3,0:T(8,128)S(1)} %copy.114), channel_id=1, source_target_pairs={{0,16},{16,32},{32,48},{48,64},{64,80},{80,96},{96,112},{112,128},... | collective-permute-start | bytes 98312 | tf_op jit(solution)/shard_map/ppermute | solution.py:13
  108.9 30.4 %collective-permute-start.11 = (f32[16,16,16,2]{2,1,3,0:T(8,128)}, f32[16,16,16,2]{2,1,3,0:T(8,128)}, u32[]{:S(2)}, u32[]{:S(2)}) collective-permute-start(f32[16,16,16,2]{2,1,3,0:T(8,128)} %copy.117), channel_id=1, source_target_pairs={{16,0},{32,16},{48,32},{64,48},{80,64},{96,80},{112,96},{128,112},... | collective-permute-start | bytes 98312 | tf_op jit(solution)/shard_map/ppermute | solution.py:13
  110.2 24.9 %collective-permute-start.8 = (f32[16,16,2,16]{3,2,1,0:T(2,128)}, f32[16,16,2,16]{3,2,1,0:T(2,128)}, u32[]{:S(2)}, u32[]{:S(2)}) collective-permute-start(f32[16,16,2,16]{3,2,1,0:T(2,128)} %get-tuple-element.25), channel_id=1, source_target_pairs={{0,32},{16,48},{32,64},{48,80},{64,96},{80,112},{96,128},{112,144}... | collective-permute-start | bytes 98312 | tf_op jit(solution)/shard_map/ppermute | solution.py:13
  114.2 23.1 %collective-permute-start.9 = (f32[16,16,2,16]{3,2,1,0:T(2,128)}, f32[16,16,2,16]{3,2,1,0:T(2,128)}, u32[]{:S(2)}, u32[]{:S(2)}) collective-permute-start(f32[16,16,2,16]{3,2,1,0:T(2,128)} %get-tuple-element.26), channel_id=1, source_target_pairs={{32,0},{48,16},{64,32},{80,48},{96,64},{112,80},{128,96},{144,112}... | collective-permute-start | bytes 98312 | tf_op jit(solution)/shard_map/ppermute | solution.py:13
  115.5 25.5 %collective-permute-start.6 = (f32[16,2,16,16]{3,2,1,0:T(8,128)}, f32[16,2,16,16]{3,2,1,0:T(8,128)}, u32[]{:S(2)}, u32[]{:S(2)}) collective-permute-start(f32[16,2,16,16]{3,2,1,0:T(8,128)} %get-tuple-element.27), channel_id=1, source_target_pairs={{0,128},{16,144},{32,160},{48,176},{64,192},{80,208},{96,224},{112... | collective-permute-start | bytes 98312 | tf_op jit(solution)/shard_map/ppermute | solution.py:13
  135.1 14.4 %collective-permute-start.7 = (f32[16,2,16,16]{3,2,1,0:T(8,128)}, f32[16,2,16,16]{3,2,1,0:T(8,128)}, u32[]{:S(2)}, u32[]{:S(2)}) collective-permute-start(f32[16,2,16,16]{3,2,1,0:T(8,128)} %get-tuple-element.28), channel_id=1, source_target_pairs={{128,0},{144,16},{160,32},{176,48},{192,64},{208,80},{224,96},{240... | collective-permute-start | bytes 98312 | tf_op jit(solution)/shard_map/ppermute | solution.py:13
  145.6 4.9 copy-start.2
  161.7 0.7 copy-start.6
  170.9 20.6 %all-to-all-start = ((f32[16,16,256]{2,0,1:T(8,128)}), f32[16,16,256]{2,0,1:T(8,128)S(1)}, u32[]{:S(2)}, u32[]{:S(2)}) async-start(f32[16,16,256]{2,0,1:T(8,128)} %bitcast.90), calls=%async_computation | async-start | bytes 524288 | tf_op jit(solution)/shard_map/all_to_all | solution.py:66
  180.0 280.2 %all-reduce.3.cloned.1.call-start = ((), (), s32[]{:S(2)}) async-start(), calls=%async_computation.2 | async-start | bytes 524288 | tf_op jit(solution)/shard_map/psum | solution.py:71
Sparse Core Ops, SparseCore 0:
  192.8 267.2 all-reduce.2
where the time goes:
time: 558 us; the launch traced here: 549 us
  waiting for transfers between devices  286 us (51%)
  other arithmetic  99.4 us (18%)
  local copies, waits for them, and re-layouts  69.6 us (12%)
  starting transfers between devices  56.5 us (10%)
  blocking collectives  17.7 us (3%)
  between operations  15.5 us (3%)
    psum x1, waiting for transfers between devices, local(): gram = lax.psum(partial_value, ('dom', 'band'))  267 us
    ppermute x12, starting transfers between devices, passed_along(): return lax.ppermute(value, axis, pairs)  47.3 us
    another operation x6, other arithmetic, local(): lower = jnp.linalg.cholesky(gram)  34 us
    another operation x4, other arithmetic, local(): rotated = jax.scipy.linalg.solve_triangular(lower, pieces, lower=True)  19.7 us
    all_to_all x1, blocking collectives, local(): lax.all_to_all(rotated, 'band', split_axis=0, concat_axis=1, tiled=True)  17.7 us
    mul x3, other arithmetic, apply_h(): return -0.5 * kinetic + potential[None, :] * values + extra  16.2 us
    slice x8, local copies, waits for them, and re-layouts, laplace(): upper_face = lax.slice_in_dim(grid, CUBE - 2, CUBE, axis=axis)  15.5 us
    scatter-add x2, other arithmetic, nonlocal_one(): jnp.zeros_like(values).at[:, points.reshape(-1)]  14.8 us
  transfers between devices with their start and end apart: 14, of which 3 were waited for; matrix products, arithmetic and copies ran while one was open for 9% of the time, Pallas kernels for 0%

commit v1 on v0

--- a/solution.py
+++ b/solution.py
@@ -68,7 +68,7 @@
     partial_value = (
         jnp.dot(pieces, pieces.T, precision=high, preferred_element_type=jnp.float32) * scale
     )
-    gram = lax.psum(partial_value, ("dom", "band"))
+    gram = lax.psum(lax.psum(partial_value, "band"), "dom")
     lower = jnp.linalg.cholesky(gram)
     rotated = jax.scipy.linalg.solve_triangular(lower, pieces, lower=True)
     return lax.all_to_all(rotated, "band", split_axis=0, concat_axis=1, tiled=True)

time: 558 us -> 563 us (level)
  blocking collectives: 17.7 us -> 43.7 us
  waiting for transfers between devices: 286 us -> 275 us
  starting transfers between devices: 56.5 us -> 47.3 us
    all_to_all x0 -> x1, blocking collectives: none -> 20.5 us  [local(): lax.all_to_all(filtered, 'band', split_axis=1, concat_axis=0, tiled=True)]
    all_to_all x1 -> x0, waiting for transfers between devices: 11.3 us -> none  [local(): lax.all_to_all(filtered, 'band', split_axis=1, concat_axis=0, tiled=True)]
    all_to_all x1 -> x0, starting transfers between devices: 9.01 us -> none  [local(): lax.all_to_all(filtered, 'band', split_axis=1, concat_axis=0, tiled=True)]
    psum x1 -> x2, waiting for transfers between devices: 267 us -> 268 us  [local(): gram = lax.psum(lax.psum(partial_value, 'band'), 'dom')]
where the time goes in v1:
time: 563 us; the launch traced here: 554 us
  waiting for transfers between devices  275 us (49%)
  other arithmetic  99.4 us (18%)
  local copies, waits for them, and re-layouts  68.6 us (12%)
  starting transfers between devices  47.3 us (8%)
  blocking collectives  43.7 us (8%)
  between operations  15.4 us (3%)
    psum x2, waiting for transfers between devices, local(): gram = lax.psum(lax.psum(partial_value, 'band'), 'dom')  268 us
    ppermute x12, starting transfers between devices, passed_along(): return lax.ppermute(value, axis, pairs)  47.3 us
    another operation x6, other arithmetic, local(): lower = jnp.linalg.cholesky(gram)  33.9 us
    all_to_all x1, blocking collectives, local(): lax.all_to_all(rotated, 'band', split_axis=0, concat_axis=1, tiled=True)  23.1 us
    all_to_all x1, blocking collectives, local(): lax.all_to_all(filtered, 'band', split_axis=1, concat_axis=0, tiled=True)  20.5 us
    another operation x4, other arithmetic, local(): rotated = jax.scipy.linalg.solve_triangular(lower, pieces, lower=True)  19.7 us
    mul x3, other arithmetic, apply_h(): return -0.5 * kinetic + potential[None, :] * values + extra  16.3 us
    slice x8, local copies, waits for them, and re-layouts, laplace(): upper_face = lax.slice_in_dim(grid, CUBE - 2, CUBE, axis=axis)  15.5 us
  transfers between devices with their start and end apart: 14, of which 3 were waited for; matrix products, arithmetic and copies ran while one was open for 9% of the time, Pallas kernels for 0%

profile of v1, /device:TPU:1, one launch (start us, length us, event | category | flops | bytes accessed | tf_op | source)
XLA Modules:
  0.0 553.6 jit_solution(16830958679058016174)
XLA Ops:
  14.0 4.7 collective-permute-start.4
  18.7 3.9 copy.105
  25.1 5.5 %collective-permute-start.2 = (f32[16,16,2,16]{3,2,1,0:T(2,128)}, f32[16,16,2,16]{3,2,1,0:T(2,128)}, u32[]{:S(2)}, u32[]{:S(2)}) collective-permute-start(f32[16,16,2,16]{3,2,1,0:T(2,128)} %get-tuple-element.31), channel_id=1, source_target_pairs={{0,32},{16,48},{32,64},{48,80},{64,96},{80,112},{96,128},{112,144}... | collective-permute-start | bytes 98312 | tf_op jit(solution)/shard_map/ppermute | solution.py:13
  32.9 9.7 %collective-permute-start = (f32[16,2,16,16]{3,2,1,0:T(8,128)}, f32[16,2,16,16]{3,2,1,0:T(8,128)}, u32[]{:S(2)}, u32[]{:S(2)}) collective-permute-start(f32[16,2,16,16]{3,2,1,0:T(8,128)} %get-tuple-element.33), channel_id=1, source_target_pairs={{0,128},{16,144},{32,160},{48,176},{64,192},{80,208},{96,224},{112... | collective-permute-start | bytes 98312 | tf_op jit(solution)/shard_map/ppermute | solution.py:13
  44.6 4.4 gather_fusion
  64.2 7.2 %collective-permute-done.1 = f32[16,2,16,16]{3,2,1,0:T(8,128)} collective-permute-done((f32[16,2,16,16]{3,2,1,0:T(8,128)}, f32[16,2,16,16]{3,2,1,0:T(8,128)}, u32[]{:S(2)}, u32[]{:S(2)}) %collective-permute-start.1) | collective-permute-done | bytes 32800 | tf_op jit(solution)/shard_map/ppermute | solution.py:13
  72.4 8.2 %fusion.20 = f32[16,16,16,16]{3,2,1,0:T(8,128)} fusion(f32[16,16,16,16]{3,2,1,0:T(8,128)S(1)} %reshape.78, f32[16,2,16,16]{3,2,1,0:T(8,128)S(1)} %broadcast_multiply_fusion.10, f32[16,2,16,16]{3,2,1,0:T(8,128)S(1)} %broadcast_multiply_fusion.12, f32[16,16,2,16]{3,2,1,0:T(2,128)S(1)} %bitcast.110, f32[16,16,2,16]{3,2,1,0:T(2,128)S(1)} %bitcast.108, ...), kind=kLoop, calls=%fused_computation.42 | loop fusion | flops 2097152 | bytes 720896 | tf_op jit(solution)/shard_map/mul | solution.py:62
  84.3 7.6 %scatter_fusion = f32[16,4096]{0,1:T(8,128)S(1)} fusion(f32[16,4096]{0,1:T(8,128)S(1)} %copy.111, s32[1024]{0:T(1024)S(1)} %bitcast.122, f32[1024,16]{1,0:T(8,128)} %copy.112), kind=kCustom, calls=%fused_computation.2 | custom fusion | flops 16384 | bytes 200704 | tf_op jit(solution)/shard_map/scatter-add | solution.py:44
  105.1 3.9 copy.117
  110.2 4.1 collective-permute-start.8
  115.6 13.3 %collective-permute-start.6 = (f32[16,2,16,16]{3,2,1,0:T(8,128)}, f32[16,2,16,16]{3,2,1,0:T(8,128)}, u32[]{:S(2)}, u32[]{:S(2)}) collective-permute-start(f32[16,2,16,16]{3,2,1,0:T(8,128)} %get-tuple-element.27), channel_id=1, source_target_pairs={{0,128},{16,144},{32,160},{48,176},{64,192},{80,208},{96,224},{112... | collective-permute-start | bytes 98312 | tf_op jit(solution)/shard_map/ppermute | solution.py:13
  128.9 4.4 gather_fusion.1
  145.6 3.9 copy.119
  150.5 8.2 %fusion.9 = f32[16,16,16,16]{3,2,1,0:T(8,128)} fusion(f32[16,16,16,16]{3,2,1,0:T(8,128)S(1)} %reshape.81, f32[16,2,16,16]{3,2,1,0:T(8,128)S(1)} %broadcast_multiply_fusion.9, f32[16,2,16,16]{3,2,1,0:T(8,128)S(1)} %copy-done.2, f32[16,16,2,16]{3,2,1,0:T(2,128)S(1)} %bitcast.109, f32[16,16,2,16]{3,2,1,0:T(2,128)S(1)} %bitcast.107, ...), kind=kLoop, calls=%fused_computation.31 | loop fusion | flops 2097152 | bytes 720896 | tf_op jit(solution)/shard_map/mul | solution.py:62
  162.5 7.2 %scatter_fusion.1 = f32[16,4096]{0,1:T(8,128)S(1)} fusion(f32[16,4096]{0,1:T(8,128)S(1)} %copy.123, s32[1024]{0:T(1024)S(1)} %bitcast.123, f32[1024,16]{1,0:T(8,128)} %copy.124), kind=kCustom, calls=%fused_computation.3 | custom fusion | flops 16384 | bytes 200704 | tf_op jit(solution)/shard_map/scatter-add | solution.py:44
  170.4 20.5 %all_to_all.38 = f32[16,16,256]{2,0,1:T(8,128)S(1)} all-to-all(f32[16,16,256]{2,0,1:T(8,128)S(1)} %bitcast.112), channel_id=1, replica_groups=mesh['dom'=32,'band'=16] {'band'}, dimensions={1} | all-to-all | bytes 524288 | tf_op jit(solution)/shard_map/all_to_all | solution.py:66
  192.1 111.0 %all-reduce.4.cloned.1.call-done = f32[256,256]{0,1:T(8,128)} async-done(((f32[256,256]{0,1:T(8,128)}), f32[256,256]{0,1:T(8,128)}) %all-reduce.4.cloned.1.call-update) | async-done | bytes 262160 | tf_op jit(solution)/shard_map/psum | solution.py:71
  303.2 157.0 %all-reduce.6.cloned.1.call-done = f32[256,256]{0,1:T(8,128)} async-done(((f32[256,256]{0,1:T(8,128)}), f32[256,256]{0,1:T(8,128)}) %all-reduce.6.cloned.1.call-update) | async-done | bytes 262160 | tf_op jit(solution)/shard_map/psum | solution.py:71
  462.3 11.7 %cholesky.50 = f32[128,128]{1,0:T(8,128)S(1)} custom-call(f32[128,128]{1,0:T(8,128)S(1)} %cholesky.118), custom_call_target="Cholesky" | custom-call | tf_op jit(solution)/shard_map/jit(cholesky)/cholesky | solution.py:72
  474.0 9.8 %custom-call.15 = f32[1,128,128]{1,2,0:T(8,128)S(1)} custom-call(f32[1,128,128]{2,1,0:T(8,128)S(1)} %get-tuple-element.40), custom_call_target="InvertDiagBlocksLowerTriangular" | custom-call | tf_op jit(solution)/shard_map/jit(cholesky)/cholesky | solution.py:72
  484.3 11.7 %cholesky.105 = f32[128,128]{1,0:T(8,128)S(1)} custom-call(f32[128,128]{1,0:T(8,128)S(1)} %convolution_subtract_fusion.1), custom_call_target="Cholesky" | custom-call | tf_op jit(solution)/shard_map/jit(cholesky)/cholesky | solution.py:72
  498.0 4.0 while.1
  502.0 19.7 %custom-call.16 = f32[2,128,128]{1,2,0:T(8,128)S(1)} custom-call(f32[2,128,128]{2,1,0:T(8,128)S(1)} %get-tuple-element.12), custom_call_target="InvertDiagBlocksLowerTriangular" | custom-call | tf_op jit(solution)/shard_map/jit(_solve_triangular)/triangular_solve | solution.py:73
  522.7 23.1 %all_to_all.39 = f32[16,16,256]{2,1,0:T(8,128)S(1)} all-to-all(f32[16,16,256]{2,1,0:T(8,128)S(1)} %bitcast.111), channel_id=1, replica_groups=mesh['dom'=32,'band'=16] {'band'}, dimensions={0} | all-to-all | bytes 524288 | tf_op jit(solution)/shard_map/all_to_all | solution.py:74
  (124 shorter events, 77.3 us)
Async XLA Ops:
  6.5 43.2 %copy-start = (f32[4,8,256]{2,1,0:T(8,128)S(1)}, f32[4,8,256]{2,1,0:T(8,128)}, u32[]{:S(2)}) copy-start(f32[4,8,256]{2,1,0:T(8,128)} %param.8) | copy-start | bytes 98308
  6.5 296.6 %all-reduce.4.cloned.1.call-start = ((), (), s32[]{:S(2)}) async-start(), calls=%async_computation.2 | async-start | bytes 524288 | tf_op jit(solution)/shard_map/psum | solution.py:71
  14.0 39.8 %collective-permute-start.4 = (f32[16,16,16,2]{2,1,3,0:T(8,128)S(1)}, f32[16,16,16,2]{2,1,3,0:T(8,128)}, u32[]{:S(2)}, u32[]{:S(2)}) collective-permute-start(f32[16,16,16,2]{2,1,3,0:T(8,128)S(1)} %copy.102), channel_id=1, source_target_pairs={{0,16},{16,32},{32,48},{48,64},{64,80},{80,96},{96,112},{112,128},... | collective-permute-start | bytes 98312 | tf_op jit(solution)/shard_map/ppermute | solution.py:13
  18.7 23.9 %copy-start.1 = (f32[16,4096]{1,0:T(8,128)S(1)}, f32[16,4096]{1,0:T(8,128)}, u32[]{:S(2)}) copy-start(f32[16,4096]{1,0:T(8,128)} %param.5) | copy-start | bytes 786436
  22.6 21.9 %copy-start.9 = (s32[4,256]{1,0:T(4,128)S(1)}, s32[4,256]{1,0:T(4,128)}, u32[]{:S(2)}) copy-start(s32[4,256]{1,0:T(4,128)} %param.7) | copy-start | bytes 12292
  22.6 32.2 %collective-permute-start.5 = (f32[16,16,16,2]{2,1,3,0:T(8,128)}, f32[16,16,16,2]{2,1,3,0:T(8,128)}, u32[]{:S(2)}, u32[]{:S(2)}) collective-permute-start(f32[16,16,16,2]{2,1,3,0:T(8,128)} %copy.105), channel_id=1, source_target_pairs={{16,0},{32,16},{48,32},{64,48},{80,64},{96,80},{112,96},{128,112},... | collective-permute-start | bytes 98312 | tf_op jit(solution)/shard_map/ppermute | solution.py:13
  25.1 26.4 %collective-permute-start.2 = (f32[16,16,2,16]{3,2,1,0:T(2,128)}, f32[16,16,2,16]{3,2,1,0:T(2,128)}, u32[]{:S(2)}, u32[]{:S(2)}) collective-permute-start(f32[16,16,2,16]{3,2,1,0:T(2,128)} %get-tuple-element.31), channel_id=1, source_target_pairs={{0,32},{16,48},{32,64},{48,80},{64,96},{80,112},{96,128},{112,144}... | collective-permute-start | bytes 98312 | tf_op jit(solution)/shard_map/ppermute | solution.py:13
  30.6 19.1 %copy-start.4 = (f32[4096]{0:T(1024)S(1)}, f32[4096]{0:T(1024)}, u32[]{:S(2)}) copy-start(f32[4096]{0:T(1024)} %param.6) | copy-start | bytes 49156
  30.6 23.1 %collective-permute-start.3 = (f32[16,16,2,16]{3,2,1,0:T(2,128)}, f32[16,16,2,16]{3,2,1,0:T(2,128)S(1)}, u32[]{:S(2)}, u32[]{:S(2)}) collective-permute-start(f32[16,16,2,16]{3,2,1,0:T(2,128)} %get-tuple-element.32), channel_id=1, source_target_pairs={{32,0},{48,16},{64,32},{80,48},{96,64},{112,80},{128,96},{144,112}... | collective-permute-start | bytes 98312 | tf_op jit(solution)/shard_map/ppermute | solution.py:13
  32.9 17.1 %copy-start.3 = (f32[4,8,8]{2,1,0:T(8,128)S(1)}, f32[4,8,8]{2,1,0:T(8,128)}, u32[]{:S(2)}) copy-start(f32[4,8,8]{2,1,0:T(8,128)} %param.9) | copy-start | bytes 3076
  32.9 23.6 %collective-permute-start = (f32[16,2,16,16]{3,2,1,0:T(8,128)}, f32[16,2,16,16]{3,2,1,0:T(8,128)}, u32[]{:S(2)}, u32[]{:S(2)}) collective-permute-start(f32[16,2,16,16]{3,2,1,0:T(8,128)} %get-tuple-element.33), channel_id=1, source_target_pairs={{0,128},{16,144},{32,160},{48,176},{64,192},{80,208},{96,224},{112... | collective-permute-start | bytes 98312 | tf_op jit(solution)/shard_map/ppermute | solution.py:13
  44.6 4.6 copy-start.7
  51.5 19.9 %collective-permute-start.1 = (f32[16,2,16,16]{3,2,1,0:T(8,128)}, f32[16,2,16,16]{3,2,1,0:T(8,128)}, u32[]{:S(2)}, u32[]{:S(2)}) collective-permute-start(f32[16,2,16,16]{3,2,1,0:T(8,128)} %get-tuple-element.34), channel_id=1, source_target_pairs={{128,0},{144,16},{160,32},{176,48},{192,64},{208,80},{224,96},{240... | collective-permute-start | bytes 98312 | tf_op jit(solution)/shard_map/ppermute | solution.py:13
  83.7 0.7 copy-start.5
  99.9 29.0 %copy-start.8 = (s32[1024]{0:T(1024)S(1)}, s32[1024]{0:T(1024)}, u32[]{:S(2)}) copy-start(s32[1024]{0:T(1024)} %copy-done.7) | copy-start | bytes 12292
  103.1 35.3 %collective-permute-start.10 = (f32[16,16,16,2]{2,1,3,0:T(8,128)S(1)}, f32[16,16,16,2]{2,1,3,0:T(8,128)}, u32[]{:S(2)}, u32[]{:S(2)}) collective-permute-start(f32[16,16,16,2]{2,1,3,0:T(8,128)S(1)} %copy.114), channel_id=1, source_target_pairs={{0,16},{16,32},{32,48},{48,64},{64,80},{80,96},{96,112},{112,128},... | collective-permute-start | bytes 98312 | tf_op jit(solution)/shard_map/ppermute | solution.py:13
  109.0 30.4 %collective-permute-start.11 = (f32[16,16,16,2]{2,1,3,0:T(8,128)}, f32[16,16,16,2]{2,1,3,0:T(8,128)}, u32[]{:S(2)}, u32[]{:S(2)}) collective-permute-start(f32[16,16,16,2]{2,1,3,0:T(8,128)} %copy.117), channel_id=1, source_target_pairs={{16,0},{32,16},{48,32},{64,48},{80,64},{96,80},{112,96},{128,112},... | collective-permute-start | bytes 98312 | tf_op jit(solution)/shard_map/ppermute | solution.py:13
  110.2 24.9 %collective-permute-start.8 = (f32[16,16,2,16]{3,2,1,0:T(2,128)}, f32[16,16,2,16]{3,2,1,0:T(2,128)}, u32[]{:S(2)}, u32[]{:S(2)}) collective-permute-start(f32[16,16,2,16]{3,2,1,0:T(2,128)} %get-tuple-element.25), channel_id=1, source_target_pairs={{0,32},{16,48},{32,64},{48,80},{64,96},{80,112},{96,128},{112,144}... | collective-permute-start | bytes 98312 | tf_op jit(solution)/shard_map/ppermute | solution.py:13
  114.3 23.1 %collective-permute-start.9 = (f32[16,16,2,16]{3,2,1,0:T(2,128)}, f32[16,16,2,16]{3,2,1,0:T(2,128)}, u32[]{:S(2)}, u32[]{:S(2)}) collective-permute-start(f32[16,16,2,16]{3,2,1,0:T(2,128)} %get-tuple-element.26), channel_id=1, source_target_pairs={{32,0},{48,16},{64,32},{80,48},{96,64},{112,80},{128,96},{144,112}... | collective-permute-start | bytes 98312 | tf_op jit(solution)/shard_map/ppermute | solution.py:13
  115.6 25.5 %collective-permute-start.6 = (f32[16,2,16,16]{3,2,1,0:T(8,128)}, f32[16,2,16,16]{3,2,1,0:T(8,128)}, u32[]{:S(2)}, u32[]{:S(2)}) collective-permute-start(f32[16,2,16,16]{3,2,1,0:T(8,128)} %get-tuple-element.27), channel_id=1, source_target_pairs={{0,128},{16,144},{32,160},{48,176},{64,192},{80,208},{96,224},{112... | collective-permute-start | bytes 98312 | tf_op jit(solution)/shard_map/ppermute | solution.py:13
  135.1 14.4 %collective-permute-start.7 = (f32[16,2,16,16]{3,2,1,0:T(8,128)}, f32[16,2,16,16]{3,2,1,0:T(8,128)}, u32[]{:S(2)}, u32[]{:S(2)}) collective-permute-start(f32[16,2,16,16]{3,2,1,0:T(8,128)} %get-tuple-element.28), channel_id=1, source_target_pairs={{128,0},{144,16},{160,32},{176,48},{192,64},{208,80},{224,96},{240... | collective-permute-start | bytes 98312 | tf_op jit(solution)/shard_map/ppermute | solution.py:13
  145.6 4.9 copy-start.2
  161.8 0.7 copy-start.6
  192.0 268.1 %all-reduce.6.cloned.1.call-start = ((), (), s32[]{:S(2)}) async-start(), calls=%async_computation.3 | async-start | bytes 524288 | tf_op jit(solution)/shard_map/psum | solution.py:71
Sparse Core Ops, SparseCore 0:
  192.2 110.9 all-reduce.3
  306.6 153.5 all-reduce.5
